TPU v7x, 256 devices: a whole 4x4x8 slice. The times are simulated.
256 devices in a mesh: mp: 2 (over x_hi), lat: 8 (over x_lo, y), lon: 16 (over z, core).
Axes of the slice: x: 4 (x_hi: 2, x_lo: 2; x = x_hi * 2 + x_lo), y: 4, z: 8, core: 2. Of those that a mesh axis runs over, the one named last changes fastest.
Arguments:
- adjoint: float32 [2, 2, 72, 128, 2048], P('mp', None, None, 'lat', 'lon'), may hold values from -6 to 6
- courant: float32 [2, 2, 128, 2048], P('mp', None, 'lat', 'lon'), may hold values from 0.05 to 0.45
- diffusivity: float32 [2, 71, 128, 2048], P('mp', None, 'lat', 'lon'), may hold values from 0.005 to 0.24
- coupling: float32 [2, 128, 2048], P('mp', 'lat', 'lon'), may hold values from 0.05 to 0.45
- partner: int32 [2, 16384], P('mp', ('lat', 'lon')), may hold values from 0 to 16383, as said below
- mask: int32 [2, 128, 2048], P('mp', 'lat', 'lon'), may hold values from 0 to 1, as said below
Outputs:
- result_adjoint: float32 [2, 2, 72, 128, 2048], P('mp', None, None, 'lat', 'lon')
Inputs may be any that keep to these rules, and one draw needn't show every extreme that they name: partner[0, q] is the ocean tile coupled to atmosphere tile q and partner[1] is its inverse, tiles numbered as in the first step; the tiles of one device have partners on exactly 64 devices, 2 tiles on each. `mask`: 1 marks a cell over sea; coupled tiles carry the same flags cell by cell.
All inputs are finite; a program needn't handle non-finite values.
Results may differ from a plain program's by a relative error of at most 0.00002.
Values sent between devices are 32-bit elements; how exact they have to be, the bound alone decides.
A program may use at most 64 MiB of HBM per device.

v0:
```python
import jax
import jax.numpy as jnp
from jax import lax
from jax.sharding import PartitionSpec as P

TILE = 16
STEPS = 4


def passed_along(block, axis, distance):
    devices = range(lax.axis_size(axis))
    route = [((i - distance) % len(devices), i) for i in devices]
    return lax.ppermute(block, axis, route)


def shifted(value, axis, steps):
    count = lax.axis_size(axis)
    first, last = (max(0, -steps), min(count, count - steps))
    return lax.ppermute(value, axis, [(source, source + steps) for source in range(first, last)])


def from_partner(array, axis, apart):
    return lax.ppermute(array, axis, [(i, i ^ 1 << apart) for i in range(lax.axis_size(axis))])


def advect_local(fields, zonal, meridional, weight):
    eastward = zonal * fields
    northward = meridional * fields
    east_edge = passed_along(eastward[..., 0:1], "lon", -1)
    north_edge = shifted(northward[..., 0:1, :], "lat", -1)
    east_next = jnp.concatenate([eastward[..., 1:], east_edge], axis=-1)
    north_next = jnp.concatenate([northward[..., 1:, :], north_edge], axis=-2)
    return weight * fields + east_next + north_next


def diffuse(fields, kappa):
    fluxes = kappa * (fields[:, 1:] - fields[:, :-1])
    edge = jnp.zeros_like(fields[:, :1])
    return fields + jnp.concatenate([fluxes, edge], 1) - jnp.concatenate([edge, fluxes], 1)


def local_tiles(surface):
    tracers, rows_here, cols_here = surface.shape
    shaped = surface.reshape(tracers, rows_here, cols_here // TILE, TILE)
    return shaped.transpose(1, 2, 0, 3).reshape(rows_here * (cols_here // TILE), tracers * TILE)


def from_local_tiles(tile_rows, tracers, rows_here, cols_here):
    shaped = tile_rows.reshape(rows_here, cols_here // TILE, tracers, TILE)
    return shaped.transpose(2, 0, 1, 3).reshape(tracers, rows_here, cols_here)


def send_slots(routing, tile_count, capacity):
    target = routing // tile_count
    same_target = target[:, None] == target[None, :]
    positions = jnp.arange(tile_count, dtype=jnp.int32)
    earlier = jnp.sum(same_target & (positions[None, :] < positions[:, None]), axis=1)
    return target * capacity + earlier


def recv_slots(routing, tile_count, capacity):
    target = routing // tile_count
    local_slot = routing % tile_count
    same_target = target[:, None] == target[None, :]
    earlier = jnp.sum(same_target & (local_slot[None, :] < local_slot[:, None]), axis=1)
    return target * capacity + earlier


def local(adjoint, courant, diffusivity, coupling, partner, mask):
    fields = adjoint[0]
    zonal = courant[0, 0]
    meridional = courant[0, 1]
    weight = 1.0 - zonal - meridional
    kappa = diffusivity[0][None]
    scale_field = coupling[0]
    routing = partner[0]
    tracers, levels, rows_here, cols_here = fields.shape
    tile_count = routing.shape[0]
    groups = lax.axis_size("lat") * lax.axis_size("lon")
    capacity = max(2, 2 * tile_count // groups)
    wet_tiles = local_tiles(
        jnp.broadcast_to(mask[0].astype(jnp.float32), (tracers, rows_here, cols_here))
    )
    arrive_slot = recv_slots(routing, tile_count, capacity)
    depart_slot = send_slots(routing, tile_count, capacity)
    for step_index in range(STEPS):
        fields = diffuse(advect_local(fields, zonal, meridional, weight), kappa)
        surface = fields[:, 0]
        own_tiles = local_tiles(surface)
        scaled = local_tiles(scale_field * surface)
        empty_slots = jnp.zeros((groups * capacity, scaled.shape[1]), jnp.float32)
        buffer = empty_slots.at[depart_slot].set(scaled)
        moved_slots = lax.all_to_all(
            buffer, ("lat", "lon"), split_axis=0, concat_axis=0, tiled=True
        )
        arrived = from_partner(moved_slots, "mp", 0)
        received = arrived[arrive_slot]
        new_tiles = own_tiles + wet_tiles * (received - scaled)
        fields = fields.at[:, 0].set(from_local_tiles(new_tiles, tracers, rows_here, cols_here))
    return fields[None]


def solution(mesh):
    placed = (
        P("mp", None, None, "lat", "lon"),
        P("mp", None, "lat", "lon"),
        P("mp", None, "lat", "lon"),
        P("mp", "lat", "lon"),
        P("mp", ("lat", "lon")),
        P("mp", "lat", "lon"),
    )
    return jax.shard_map(
        local,
        mesh=mesh,
        in_specs=placed,
        out_specs=P("mp", None, None, "lat", "lon"),
        check_vma=False,
    )
```

profile of v0, /device:TPU:1, one launch (start us, length us, event | category | flops | bytes accessed | tf_op | source)
XLA Modules:
  0.0 224.2 jit_solution(15918482573997809584)
XLA Ops:
  0.9 2.2 copy.54
  4.5 3.2 %collective-permute-start = (f32[2,72,16,1]{1,2,3,0:T(8,128)}, f32[2,72,16,1]{1,2,3,0:T(8,128)S(1)}, u32[]{:S(2)}, u32[]{:S(2)}) collective-permute-start(f32[2,72,16,1]{1,2,3,0:T(8,128)} %slice.229), channel_id=1, source_target_pairs={{1,0},{2,1},{3,2},{4,3},{5,4},{6,5},{7,6},{8,7},{9,8},{10,9},{11,1... | collective-permute-start | bytes 27656 | tf_op jit(solution)/shard_map/ppermute | solution.py:13
  8.4 1.3 collective-permute-start.1
  10.9 1.4 slice.228
  12.4 1.5 slice.230
  14.1 1.6 copy.57
  15.7 2.9 %fusion.4 = f32[2,72,16,128]{1,2,3,0:T(8,128)S(1)} fusion(f32[2,72,16,1]{1,2,3,0:T(8,128)S(1)} %collective-permute-done, f32[2,72,16,127]{1,2,3,0:T(8,128)} %slice.228, f32[2,72,1,128]{1,2,3,0:T(1,128)S(1)} %collective-permute-done.1, f32[2,72,15,128]{1,2,3,0:T(8,128)} %slice.230, f32[1,2,72,16,128]{2,3,4,1,0:T(8,128)S(1)} %copy.54, f32[16,128]{0,1:T(8,128)S(1)} %copy.53), kind=kLoop, calls=%fused_computation.17 | loop fusion | flops 1474560 | bytes 4726784 | tf_op jit(solution)/shard_map/add | solution.py:33
  19.9 0.8 copy.58
  21.6 1.7 reshape.389
  23.2 1.8 scatter_custom_fusion
  25.0 25.2 %all_to_all.48 = f32[128,2,32]{2,1,0:T(2,128)} all-to-all(f32[128,2,32]{2,1,0:T(2,128)} %bitcast.143), channel_id=1, replica_groups=mesh['mp'=2,'lat'=8,'lon'=16] {'lat','lon'}, dimensions={0} | all-to-all | bytes 65536 | tf_op jit(solution)/shard_map/all_to_all | solution.py:93
  50.2 2.7 %collective-permute-start.2 = (f32[256,32]{1,0:T(8,128)}, f32[256,32]{1,0:T(8,128)S(1)}, u32[]{:S(2)}, u32[]{:S(2)}) collective-permute-start(f32[256,32]{1,0:T(8,128)} %bitcast.13), channel_id=1, source_target_pairs={{0,128},{128,0},{1,129},{129,1},{2,130},{130,2},{3,131},{131,3},{4... | collective-permute-start | bytes 98312 | tf_op jit(solution)/shard_map/ppermute | solution.py:23
  54.9 1.6 collective-permute-done.2
  56.5 1.2 gather_fusion
  57.8 1.0 gather.21
  58.7 1.6 fusion.11
  60.3 1.0 reshape.347
  61.3 2.1 copy.61
  63.5 5.9 %scatter.49 = f32[2,72,16,128]{1,2,3,0:T(8,128)S(1)} dynamic-update-slice(f32[2,72,16,128]{1,2,3,0:T(8,128)S(1)} %pad_subtract_fusion.3, f32[2,1,16,128]{1,2,3,0:T(8,128)} %copy.61, s32[]{:T(128)} %constant.123.clone.1, s32[]{:T(128)} %constant.123.clone.1, s32[]{:T(128)} %constant.123.clone.1, s32[]{:T(128)} %constant.123.clone.1) | dynamic-update-slice | bytes 32772 | tf_op jit(solution)/shard_map/scatter | solution.py:99
  70.2 1.5 collective-permute-start.4
  71.7 1.3 collective-permute-start.3
  73.3 1.6 collective-permute-done.3
  74.9 1.0 collective-permute-done.4
  77.8 0.8 copy.62
  79.5 1.7 reshape.397
  81.1 1.8 scatter_custom_fusion.1
  82.9 20.6 %all_to_all.49 = f32[128,2,32]{2,1,0:T(2,128)S(1)} all-to-all(f32[128,2,32]{2,1,0:T(2,128)} %bitcast.144), channel_id=1, replica_groups=mesh['mp'=2,'lat'=8,'lon'=16] {'lat','lon'}, dimensions={0} | all-to-all | bytes 65536 | tf_op jit(solution)/shard_map/all_to_all | solution.py:93
  103.5 2.7 %collective-permute-start.5 = (f32[256,32]{1,0:T(8,128)S(1)}, f32[256,32]{1,0:T(8,128)S(1)}, u32[]{:S(2)}, u32[]{:S(2)}) collective-permute-start(f32[256,32]{1,0:T(8,128)S(1)} %bitcast.146), channel_id=1, source_target_pairs={{0,128},{128,0},{1,129},{129,1},{2,130},{130,2},{3,131},{131,3},{4... | collective-permute-start | bytes 98312 | tf_op jit(solution)/shard_map/ppermute | solution.py:23
  106.2 3.4 %collective-permute-done.5 = f32[256,32]{1,0:T(8,128)S(1)} collective-permute-done((f32[256,32]{1,0:T(8,128)S(1)}, f32[256,32]{1,0:T(8,128)S(1)}, u32[]{:S(2)}, u32[]{:S(2)}) %collective-permute-start.5) | collective-permute-done | bytes 32800 | tf_op jit(solution)/shard_map/ppermute | solution.py:23
  109.7 1.4 gather_fusion.1
  111.0 1.0 gather.23
  112.0 1.6 fusion.10
  113.6 1.0 reshape.349
  114.6 2.1 copy.65
  116.7 5.9 %scatter.51 = f32[2,72,16,128]{1,2,3,0:T(8,128)S(1)} dynamic-update-slice(f32[2,72,16,128]{1,2,3,0:T(8,128)S(1)} %pad_subtract_fusion.2, f32[2,1,16,128]{1,2,3,0:T(8,128)} %copy.65, s32[]{:T(128)} %constant.123.clone.1, s32[]{:T(128)} %constant.123.clone.1, s32[]{:T(128)} %constant.123.clone.1, s32[]{:T(128)} %constant.123.clone.1) | dynamic-update-slice | bytes 32772 | tf_op jit(solution)/shard_map/scatter | solution.py:99
  123.4 1.3 collective-permute-start.7
  124.7 1.3 collective-permute-start.6
  126.3 1.7 collective-permute-done.6
  128.0 1.1 collective-permute-done.7
  131.0 0.8 copy.66
  132.7 1.7 reshape.405
  134.4 1.8 scatter_custom_fusion.2
  136.2 20.6 %all_to_all.50 = f32[128,2,32]{2,1,0:T(2,128)S(1)} all-to-all(f32[128,2,32]{2,1,0:T(2,128)} %bitcast.145), channel_id=1, replica_groups=mesh['mp'=2,'lat'=8,'lon'=16] {'lat','lon'}, dimensions={0} | all-to-all | bytes 65536 | tf_op jit(solution)/shard_map/all_to_all | solution.py:93
  156.7 2.7 %collective-permute-start.8 = (f32[256,32]{1,0:T(8,128)S(1)}, f32[256,32]{1,0:T(8,128)S(1)}, u32[]{:S(2)}, u32[]{:S(2)}) collective-permute-start(f32[256,32]{1,0:T(8,128)S(1)} %bitcast.147), channel_id=1, source_target_pairs={{0,128},{128,0},{1,129},{129,1},{2,130},{130,2},{3,131},{131,3},{4... | collective-permute-start | bytes 98312 | tf_op jit(solution)/shard_map/ppermute | solution.py:23
  159.5 3.4 %collective-permute-done.8 = f32[256,32]{1,0:T(8,128)S(1)} collective-permute-done((f32[256,32]{1,0:T(8,128)S(1)}, f32[256,32]{1,0:T(8,128)S(1)}, u32[]{:S(2)}, u32[]{:S(2)}) %collective-permute-start.8) | collective-permute-done | bytes 32800 | tf_op jit(solution)/shard_map/ppermute | solution.py:23
  162.9 1.4 gather_fusion.2
  164.3 1.0 gather.25
  165.2 1.6 fusion.9
  166.8 1.0 reshape.351
  167.8 2.1 copy.69
  169.9 5.9 %scatter.53 = f32[2,72,16,128]{1,2,3,0:T(8,128)S(1)} dynamic-update-slice(f32[2,72,16,128]{1,2,3,0:T(8,128)S(1)} %pad_subtract_fusion.1, f32[2,1,16,128]{1,2,3,0:T(8,128)} %copy.69, s32[]{:T(128)} %constant.123.clone.1, s32[]{:T(128)} %constant.123.clone.1, s32[]{:T(128)} %constant.123.clone.1, s32[]{:T(128)} %constant.123.clone.1) | dynamic-update-slice | bytes 32772 | tf_op jit(solution)/shard_map/scatter | solution.py:99
  176.7 1.3 collective-permute-start.10
  178.0 1.3 collective-permute-start.9
  179.6 1.7 collective-permute-done.9
  181.3 1.1 collective-permute-done.10
  184.3 0.8 copy.70
  185.4 1.0 scatter_custom_fusion.3
  186.5 20.4 %all_to_all.51 = f32[128,2,32]{2,1,0:T(2,128)S(1)} all-to-all(f32[128,2,32]{2,1,0:T(2,128)S(1)} %bitcast.142), channel_id=1, replica_groups=mesh['mp'=2,'lat'=8,'lon'=16] {'lat','lon'}, dimensions={0} | all-to-all | bytes 65536 | tf_op jit(solution)/shard_map/all_to_all | solution.py:93
  206.9 2.7 %collective-permute-start.11 = (f32[256,32]{1,0:T(8,128)S(1)}, f32[256,32]{1,0:T(8,128)S(1)}, u32[]{:S(2)}, u32[]{:S(2)}) collective-permute-start(f32[256,32]{1,0:T(8,128)S(1)} %bitcast.148), channel_id=1, source_target_pairs={{0,128},{128,0},{1,129},{129,1},{2,130},{130,2},{3,131},{131,3},{4... | collective-permute-start | bytes 98312 | tf_op jit(solution)/shard_map/ppermute | solution.py:23
  209.6 3.4 %collective-permute-done.11 = f32[256,32]{1,0:T(8,128)S(1)} collective-permute-done((f32[256,32]{1,0:T(8,128)S(1)}, f32[256,32]{1,0:T(8,128)S(1)}, u32[]{:S(2)}, u32[]{:S(2)}) %collective-permute-start.11) | collective-permute-done | bytes 32800 | tf_op jit(solution)/shard_map/ppermute | solution.py:23
  213.1 0.8 gather_fusion.3
  214.1 2.1 copy.73
  216.2 5.9 %scatter.55 = f32[1,2,72,16,128]{2,3,4,1,0:T(8,128)S(1)} dynamic-update-slice(f32[1,2,72,16,128]{2,3,4,1,0:T(8,128)S(1)} %bitcast.140, f32[1,2,1,16,128]{2,3,4,1,0:T(8,128)} %copy.73, s32[]{:T(128)} %constant.123.clone.1, s32[]{:T(128)} %constant.123.clone.1, s32[]{:T(128)} %constant.123.clone.1, s32[]{:T(128)} %constant.123.clone.1, s32[]{:T(128)} %constant.123.clone.1) | dynamic-update-slice | bytes 32772 | tf_op jit(solution)/shard_map/scatter | solution.py:99
  222.1 2.0 copy.74
  (74 shorter events, 19.8 us)
Async XLA Ops:
  3.1 6.5 %copy-start.6 = (s32[1,128]{1,0:T(1,128)S(1)}, s32[1,128]{1,0:T(1,128)}, u32[]{:S(2)}) copy-start(s32[1,128]{1,0:T(1,128)} %param.18) | copy-start | bytes 1540
  4.5 11.3 %collective-permute-start = (f32[2,72,16,1]{1,2,3,0:T(8,128)}, f32[2,72,16,1]{1,2,3,0:T(8,128)S(1)}, u32[]{:S(2)}, u32[]{:S(2)}) collective-permute-start(f32[2,72,16,1]{1,2,3,0:T(8,128)} %slice.229), channel_id=1, source_target_pairs={{1,0},{2,1},{3,2},{4,3},{5,4},{6,5},{7,6},{8,7},{9,8},{10,9},{11,1... | collective-permute-start | bytes 27656 | tf_op jit(solution)/shard_map/ppermute | solution.py:13
  8.4 7.3 %collective-permute-start.1 = (f32[2,72,1,128]{1,2,3,0:T(1,128)}, f32[2,72,1,128]{1,2,3,0:T(1,128)S(1)}, u32[]{:S(2)}, u32[]{:S(2)}) collective-permute-start(f32[2,72,1,128]{1,2,3,0:T(1,128)} %slice.231), channel_id=1, source_target_pairs={{16,0},{32,16},{48,32},{64,48},{80,64},{96,80},{112,96},{17,1},{33... | collective-permute-start | bytes 221192 | tf_op jit(solution)/shard_map/ppermute | solution.py:19
  12.4 1.6 copy-start.5
  20.8 29.4 %copy-start.1 = (f32[2,16,8,16]{3,2,1,0:T(8,128)}, f32[2,16,8,16]{3,2,1,0:T(8,128)S(1)}, u32[]{:S(2)}) copy-start(f32[2,16,8,16]{3,2,1,0:T(8,128)S(1)} %reshape_squeeze.12) | copy-start | bytes 49156
  50.2 6.4 %collective-permute-start.2 = (f32[256,32]{1,0:T(8,128)}, f32[256,32]{1,0:T(8,128)S(1)}, u32[]{:S(2)}, u32[]{:S(2)}) collective-permute-start(f32[256,32]{1,0:T(8,128)} %bitcast.13), channel_id=1, source_target_pairs={{0,128},{128,0},{1,129},{129,1},{2,130},{130,2},{3,131},{131,3},{4... | collective-permute-start | bytes 98312 | tf_op jit(solution)/shard_map/ppermute | solution.py:23
  53.5 15.9 %copy-start.4 = (s32[1024]{0:T(1024)}, s32[1024]{0:T(1024)S(1)}, u32[]{:S(2)}) copy-start(s32[1024]{0:T(1024)S(1)} %pad_clamp_fusion) | copy-start | bytes 12292
  70.2 5.7 %collective-permute-start.4 = (f32[2,72,1,128]{1,2,3,0:T(1,128)S(1)}, f32[2,72,1,128]{1,2,3,0:T(1,128)S(1)}, u32[]{:S(2)}, u32[]{:S(2)}) collective-permute-start(f32[2,72,1,128]{1,2,3,0:T(1,128)S(1)} %slice.238), channel_id=1, source_target_pairs={{16,0},{32,16},{48,32},{64,48},{80,64},{96,80},{112,96},{17,1},{33... | collective-permute-start | bytes 221192 | tf_op jit(solution)/shard_map/ppermute | solution.py:19
  71.7 3.2 %collective-permute-start.3 = (f32[2,72,16,1]{1,2,3,0:T(8,128)S(1)}, f32[2,72,16,1]{1,2,3,0:T(8,128)S(1)}, u32[]{:S(2)}, u32[]{:S(2)}) collective-permute-start(f32[2,72,16,1]{1,2,3,0:T(8,128)S(1)} %slice.236), channel_id=1, source_target_pairs={{1,0},{2,1},{3,2},{4,3},{5,4},{6,5},{7,6},{8,7},{9,8},{10,9},{11,1... | collective-permute-start | bytes 27656 | tf_op jit(solution)/shard_map/ppermute | solution.py:13
  78.7 24.8 %copy-start.2 = (f32[2,16,8,16]{3,2,1,0:T(8,128)}, f32[2,16,8,16]{3,2,1,0:T(8,128)S(1)}, u32[]{:S(2)}) copy-start(f32[2,16,8,16]{3,2,1,0:T(8,128)S(1)} %reshape_squeeze.13) | copy-start | bytes 49156
  103.5 6.2 %collective-permute-start.5 = (f32[256,32]{1,0:T(8,128)S(1)}, f32[256,32]{1,0:T(8,128)S(1)}, u32[]{:S(2)}, u32[]{:S(2)}) collective-permute-start(f32[256,32]{1,0:T(8,128)S(1)} %bitcast.146), channel_id=1, source_target_pairs={{0,128},{128,0},{1,129},{129,1},{2,130},{130,2},{3,131},{131,3},{4... | collective-permute-start | bytes 98312 | tf_op jit(solution)/shard_map/ppermute | solution.py:23
  123.4 5.7 %collective-permute-start.7 = (f32[2,72,1,128]{1,2,3,0:T(1,128)S(1)}, f32[2,72,1,128]{1,2,3,0:T(1,128)S(1)}, u32[]{:S(2)}, u32[]{:S(2)}) collective-permute-start(f32[2,72,1,128]{1,2,3,0:T(1,128)S(1)} %slice.245), channel_id=1, source_target_pairs={{16,0},{32,16},{48,32},{64,48},{80,64},{96,80},{112,96},{17,1},{33... | collective-permute-start | bytes 221192 | tf_op jit(solution)/shard_map/ppermute | solution.py:19
  124.7 3.3 %collective-permute-start.6 = (f32[2,72,16,1]{1,2,3,0:T(8,128)S(1)}, f32[2,72,16,1]{1,2,3,0:T(8,128)S(1)}, u32[]{:S(2)}, u32[]{:S(2)}) collective-permute-start(f32[2,72,16,1]{1,2,3,0:T(8,128)S(1)} %slice.243), channel_id=1, source_target_pairs={{1,0},{2,1},{3,2},{4,3},{5,4},{6,5},{7,6},{8,7},{9,8},{10,9},{11,1... | collective-permute-start | bytes 27656 | tf_op jit(solution)/shard_map/ppermute | solution.py:13
  131.9 24.8 %copy-start.3 = (f32[2,16,8,16]{3,2,1,0:T(8,128)}, f32[2,16,8,16]{3,2,1,0:T(8,128)S(1)}, u32[]{:S(2)}) copy-start(f32[2,16,8,16]{3,2,1,0:T(8,128)S(1)} %reshape_squeeze.14) | copy-start | bytes 49156
  156.7 6.2 %collective-permute-start.8 = (f32[256,32]{1,0:T(8,128)S(1)}, f32[256,32]{1,0:T(8,128)S(1)}, u32[]{:S(2)}, u32[]{:S(2)}) collective-permute-start(f32[256,32]{1,0:T(8,128)S(1)} %bitcast.147), channel_id=1, source_target_pairs={{0,128},{128,0},{1,129},{129,1},{2,130},{130,2},{3,131},{131,3},{4... | collective-permute-start | bytes 98312 | tf_op jit(solution)/shard_map/ppermute | solution.py:23
  176.7 5.7 %collective-permute-start.10 = (f32[2,72,1,128]{1,2,3,0:T(1,128)S(1)}, f32[2,72,1,128]{1,2,3,0:T(1,128)S(1)}, u32[]{:S(2)}, u32[]{:S(2)}) collective-permute-start(f32[2,72,1,128]{1,2,3,0:T(1,128)S(1)} %slice.252), channel_id=1, source_target_pairs={{16,0},{32,16},{48,32},{64,48},{80,64},{96,80},{112,96},{17,1},{33... | collective-permute-start | bytes 221192 | tf_op jit(solution)/shard_map/ppermute | solution.py:19
  178.0 3.3 %collective-permute-start.9 = (f32[2,72,16,1]{1,2,3,0:T(8,128)S(1)}, f32[2,72,16,1]{1,2,3,0:T(8,128)S(1)}, u32[]{:S(2)}, u32[]{:S(2)}) collective-permute-start(f32[2,72,16,1]{1,2,3,0:T(8,128)S(1)} %slice.250), channel_id=1, source_target_pairs={{1,0},{2,1},{3,2},{4,3},{5,4},{6,5},{7,6},{8,7},{9,8},{10,9},{11,1... | collective-permute-start | bytes 27656 | tf_op jit(solution)/shard_map/ppermute | solution.py:13
  184.3 29.7 %copy-start = (f32[16,8,16]{2,1,0:T(8,128)S(1)}, f32[16,8,16]{2,1,0:T(8,128)}, u32[]{:S(2)}) copy-start(f32[16,8,16]{2,1,0:T(8,128)} %convert_element_type.14) | copy-start | bytes 24580
  206.9 6.2 %collective-permute-start.11 = (f32[256,32]{1,0:T(8,128)S(1)}, f32[256,32]{1,0:T(8,128)S(1)}, u32[]{:S(2)}, u32[]{:S(2)}) collective-permute-start(f32[256,32]{1,0:T(8,128)S(1)} %bitcast.148), channel_id=1, source_target_pairs={{0,128},{128,0},{1,129},{129,1},{2,130},{130,2},{3,131},{131,3},{4... | collective-permute-start | bytes 98312 | tf_op jit(solution)/shard_map/ppermute | solution.py:23
where the time goes:
time: 226 us; the launch traced here: 224 us
  blocking collectives  86.7 us (38%)
  local copies, waits for them, and re-layouts  72.8 us (32%)
  starting transfers between devices  23.3 us (10%)
  other arithmetic  20.7 us (9%)
  waiting for transfers between devices  20.1 us (9%)
    all_to_all x4, blocking collectives, local(): lax.all_to_all(buffer, ('lat', 'lon'), split_axis=0, concat_axis=0, tiled...  86.7 us
    scatter x5, local copies, waits for them, and re-layouts, local(): fields.at[:, 0]  25.7 us
    ppermute x4, waiting for transfers between devices, from_partner(): lax.ppermute(array, axis, [(i, i ^ 1 << apart) for i in range(lax.axis_si...  11.9 us
    ppermute x4, starting transfers between devices, from_partner(): lax.ppermute(array, axis, [(i, i ^ 1 << apart) for i in range(lax.axis_si...  11 us
    another operation x6, local copies, waits for them, and re-layouts  9.33 us
    gather x8, local copies, waits for them, and re-layouts, local(): received = arrived[arrive_slot]  7.72 us
    ppermute x4, starting transfers between devices, passed_along(): return lax.ppermute(block, axis, route)  6.99 us
    scatter x4, local copies, waits for them, and re-layouts, local(): buffer = empty_slots.at[depart_slot].set(scaled)  6.39 us
  transfers between devices with their start and end apart: 12, of which 10 were waited for; matrix products, arithmetic and copies ran while one was open for 4% of the time, Pallas kernels for 0%

commit v1 on v0

v1 whole, which is shorter than its diff:
```python
import functools

import jax
import jax.numpy as jnp
from jax import lax
from jax.experimental import pallas as pl
from jax.experimental.pallas import tpu as pltpu
from jax.sharding import PartitionSpec as P

TILE = 16
STEPS = 4
MESH = pl.DeviceIdType.MESH
F32 = jnp.float32
BF16 = jnp.bfloat16


def hops(a, b, c):
    return (1 if a else 2) + min(b, 4 - b) + min(c, 8 - c)


OFFSETS = sorted(
    [(a, b, c, d) for a in range(2) for b in range(4) for c in range(8) for d in range(2)],
    key=lambda o: -hops(*o[:3]),
)


def iota(shape, axis):
    return lax.broadcasted_iota(jnp.int32, shape, axis)


def halves(x):
    high = x.astype(BF16)
    low = (x - high.astype(F32)).astype(BF16)
    return high, low


def dot(a, b):
    return jnp.dot(a, b, preferred_element_type=F32)


def joined(x):
    return x[:, :128] + x[:, 128:]


def kernel(
    adj, cour, diff, coup, part, msk, out,
    F, CO, KAP, CP, PT, MK, ST, STW, STS, CZE, CMN, CMS,
    ES, EE, SB, RB, SURF, NROW, BNE, OHP, OHX, LA, LB, KM, CF, ROWS,
    isem, osem, xs, xr, ns, nr, es, er, ts, tr, stage,
):
    mp, lat, lon = lax.axis_index("mp"), lax.axis_index("lat"), lax.axis_index("lon")
    me = lat * 16 + lon
    x_lo, y = lat // 4, lax.rem(lat, 4)
    z, core = lon // 2, lax.rem(lon, 2)
    east, west = (mp, lat, (lon + 1) & 15), (mp, lat, (lon + 15) & 15)
    north, south = (mp, (lat + 1) & 7, lon), (mp, (lat + 7) & 7, lon)

    loads = [
        pltpu.make_async_copy(part, PT, isem.at[0]),
        pltpu.make_async_copy(cour.at[0], CO, isem.at[1]),
        pltpu.make_async_copy(coup.at[0], CP, isem.at[2]),
        pltpu.make_async_copy(diff.at[0], KAP.at[pl.ds(0, 71)], isem.at[3]),
        pltpu.make_async_copy(msk.at[0], MK, isem.at[4]),
        pltpu.make_async_copy(adj.at[0], F.at[0, :, :, pl.ds(0, 16), :], isem.at[5]),
    ]
    bar = pltpu.get_barrier_semaphore()
    lon_peers = [(mp, lat, (lon + i) & 15) for i in (8, 9, 7, 10, 6, 11, 5, 12, 4, 13, 3, 14, 2, 15, 1)]
    lat_peers = [
        (lax.rem(mp + h, 2), (x_lo ^ a) * 4 + ((y + b) & 3), lon)
        for h in (1, 0) for a in (0, 1) for b in (2, 1, 3, 0) if h or a or b
    ]
    for peer in lat_peers + lon_peers:
        pl.semaphore_signal(bar, inc=1, device_id=peer, device_id_type=MESH)
    for load in loads:
        load.start()

    lane = iota((16, 128), 1)
    row = iota((16, 128), 0)
    sub8 = iota((8, 128), 0)
    big_lane = iota((128, 128), 1)
    big_row = iota((128, 128), 0)

    KAP[71] = jnp.zeros((16, 128), F32)
    BNE[...] = jnp.zeros((128, 128), F32)

    loads[0].wait()
    p_row = jnp.broadcast_to(PT[...], (128, 128))
    t_row = p_row // 128
    diag = big_row == big_lane
    p_col = jnp.sum(jnp.where(diag, p_row.astype(F32), 0.0), axis=1, keepdims=True)
    p_col = jnp.broadcast_to(p_col, (128, 128)).astype(jnp.int32)
    t_col, l_col = p_col // 128, p_col & 127
    same = t_row == t_col
    t_send = jnp.sum(jnp.where(big_row == (big_lane ^ 7), t_col.astype(F32), 0.0), axis=0, keepdims=True)
    t_send = jnp.broadcast_to(t_send, (128, 128))
    earlier = (t_send == t_col.astype(F32)) & (big_row < (big_lane ^ 7))
    k_send = jnp.sum(jnp.where(earlier, 1.0, 0.0), axis=0, keepdims=True)
    k_send = jnp.broadcast_to(k_send, (128, 128))
    k_arr = jnp.sum(jnp.where(same & ((p_row & 127) < l_col), 1.0, 0.0), axis=1, keepdims=True)
    KM[...] = jnp.broadcast_to(k_arr, (128, 128))
    loads[1].wait()
    loads[2].wait()
    loads[3].wait()
    a1 = CP[...] * KAP[0]
    a0 = CP[...] - a1
    ST[0:16] = a0
    ST[16:32] = a1
    ST[32:40] = jnp.where(sub8 == 0, t_send[0:8], k_send[0:8])
    CF[0] = 1.0 - CO[0] - CO[1]

    pl.semaphore_wait(bar, 30)
    statics = [
        pltpu.make_async_remote_copy(
            src_ref=src, dst_ref=dst, send_sem=ts.at[i], recv_sem=tr.at[i],
            device_id=dev, device_id_type=MESH,
        )
        for i, (src, dst, dev) in enumerate((
            (ST, STW, east), (ST, STS, north), (CO.at[0], CZE, west), (CO.at[1], CMN, south),
        ))
    ]
    for copy in statics:
        copy.start()
    for peer in lat_peers:
        pl.semaphore_signal(stage, inc=1, device_id=peer, device_id_type=MESH)

    rows_f = big_row.astype(F32)
    OHP[:, 0:128] = jnp.where((t_send == rows_f) & (k_send == 0.0), 1.0, 0.0).astype(BF16)
    OHP[:, 128:256] = jnp.where((t_send == rows_f) & (k_send == 1.0), 1.0, 0.0).astype(BF16)
    LA[0:128] = jnp.where(t_col == big_lane, 1.0, 0.0).astype(BF16)
    LA[128:256] = jnp.where(((l_col // 8) == 15) & (big_lane == t_col + 16), 1.0, 0.0).astype(BF16)
    t_east = (t_col - (t_col & 15)) + ((t_col + 1) & 15)
    LB[...] = jnp.where(((l_col & 7) == 7) & (big_lane == t_east), 1.0, 0.0).astype(BF16)

    loads[4].wait()
    CF[1] = MK[...].astype(F32)
    loads[5].wait()

    def pack_level(k, edges):
        return tuple(
            jnp.where(lane == k, pltpu.roll(F[0, t, k, 0:16, :], k, 1), edges[t]) for t in range(2)
        )

    zero = jnp.zeros((16, 128), F32)
    packed = lax.fori_loop(0, 72, pack_level, (zero, zero))
    ES[0, 0] = packed[0]
    ES[0, 1] = packed[1]

    for copy in statics:
        copy.wait()
    t_s = jnp.broadcast_to(STS[32:33], (128, 128))
    k_s = jnp.broadcast_to(STS[33:34], (128, 128))
    t_n = jnp.where(big_lane < 8, pltpu.roll(t_s, 8, 1), pltpu.roll(t_s, 16, 1))
    k_n = jnp.where(big_lane < 8, pltpu.roll(k_s, 8, 1), pltpu.roll(k_s, 16, 1))
    OHX[0:128] = jnp.where(
        (big_lane < 16) & (t_n == rows_f) & (k_n == jnp.where(big_lane < 8, 0.0, 1.0)), 1.0, 0.0
    ).astype(BF16)
    pick = big_row == 8 * (big_lane & 15)
    t_wc = jnp.sum(jnp.where(diag, jnp.broadcast_to(STW[32:33], (128, 128)), 0.0), axis=1, keepdims=True)
    k_wc = jnp.sum(jnp.where(diag, jnp.broadcast_to(STW[33:34], (128, 128)), 0.0), axis=1, keepdims=True)
    t_e = jnp.sum(jnp.where(pick, jnp.broadcast_to(t_wc, (128, 128)), 0.0), axis=0, keepdims=True)
    k_e = jnp.sum(jnp.where(pick, jnp.broadcast_to(k_wc, (128, 128)), 0.0), axis=0, keepdims=True)
    OHX[128:256] = jnp.where(
        (big_lane >= 16) & (big_lane < 48)
        & (jnp.broadcast_to(t_e, (128, 128)) == rows_f)
        & (jnp.broadcast_to(k_e, (128, 128)) == jnp.where(big_lane < 32, 0.0, 1.0)),
        1.0, 0.0,
    ).astype(BF16)
    has_south = jnp.where(lat > 0, 1.0, 0.0)
    has_north = jnp.where(lat < 7, 1.0, 0.0)
    ROWS[0] = jnp.broadcast_to(STS[15:16], (8, 128)) * has_south
    ROWS[1] = jnp.broadcast_to(STS[31:32], (8, 128)) * has_south
    CF[2] = jnp.broadcast_to(STW[0:16, 127:128], (16, 128))
    CF[3] = jnp.broadcast_to(STW[16:32, 127:128], (16, 128))
    CF[4] = jnp.broadcast_to(CZE[:, 0:1], (16, 128))
    CMS[0:16] = CO[1]
    CMS[16:24] = jnp.broadcast_to(CMN[0:1], (8, 128)) * has_north
    CF[5] = CMS[1:17]

    pl.semaphore_wait(stage, 15)

    def to_tiles(ref, rows):
        parts = []
        for t in range(2):
            full = jnp.concatenate([ref[t, pl.ds(r, 8, stride=0), :] for r in range(rows)], axis=0)
            parts.append(pltpu.roll(full, 16, 1, stride=16, stride_axis=0))
        lanes = iota((8 * rows, 128), 1)
        both = jnp.where(lanes < 16, parts[0], parts[1])
        return jnp.where(lanes < 32, both, 0.0)

    def send_surface(s):
        cz, cm = CO[0], CO[1]
        weight = CF[0]
        c0, c1 = ST[0:16], ST[16:32]
        edge = jnp.zeros((16, 128), F32)
        for t in range(2):
            f0, f1 = F[s, t, 0, 0:16, :], F[s, t, 1, 0:16, :]
            z0, z1, m0, m1 = cz * f0, cz * f1, cm * f0, cm * f1
            own = jnp.zeros((16, 128), F32)
            for c, f, zf, mf in ((c0, f0, z0, m0), (c1, f1, z1, m1)):
                east_next = jnp.where(lane == 127, 0.0, pltpu.roll(zf, 127, 1))
                north_next = jnp.where(row == 15, 0.0, pltpu.roll(mf, 15, 0))
                own += c * (weight * f + east_next + north_next)
            to_south = ROWS[0] * m0[0:8] + ROWS[1] * m1[0:8]
            SURF[t] = pltpu.roll(own, 16, 1) if t else own
            NROW[t] = pltpu.roll(to_south, 16, 1) if t else to_south
            to_west = CF[2] * z0 + CF[3] * z1
            edge = jnp.where(lane == 15 + 16 * t, pltpu.roll(to_west, 15 + 16 * t, 1), edge)
        tiles = to_tiles(SURF, 16)
        high, low = halves(tiles)
        north_tiles = pltpu.roll(to_tiles(NROW, 1), 32, 1)
        BNE[0:8] = north_tiles
        BNE[8:16] = pltpu.roll(north_tiles, 64, 1)
        BNE[16:32] = edge
        BNE[32:48] = pltpu.roll(edge, 64, 1)
        first = dot(OHP[:, 0:128], jnp.concatenate([high, low], axis=1))
        second = dot(OHP[:, 128:256], jnp.concatenate([high, low], axis=1))
        extra = dot(OHX[...], jnp.concatenate(halves(BNE[...]), axis=1))
        SB[s, 0] = joined(first) + pltpu.roll(joined(second), 64, 1) + joined(extra[0:128])
        SB[s, 1] = joined(extra[128:256])
        for a, b, c, d in OFFSETS:
            to_lat = (x_lo ^ a) * 4 + ((y + b) & 3)
            to_lon = ((z + c) & 7) * 2 + (core ^ d)
            pltpu.make_async_remote_copy(
                src_ref=SB.at[s, :, pl.ds(to_lat * 16 + to_lon, 1), :],
                dst_ref=RB.at[s, :, pl.ds(me, 1), :],
                send_sem=xs.at[s], recv_sem=xr.at[s],
                device_id=(1 - mp, to_lat, to_lon), device_id_type=MESH,
            ).start()

    def edge_copies(s):
        return (
            pltpu.make_async_remote_copy(
                src_ref=F.at[s, :, :, pl.ds(0, 1), :], dst_ref=F.at[s, :, :, pl.ds(16, 1), :],
                send_sem=ns.at[s], recv_sem=nr.at[s], device_id=south, device_id_type=MESH,
            ),
            pltpu.make_async_remote_copy(
                src_ref=ES.at[s], dst_ref=EE.at[s],
                send_sem=es.at[s], recv_sem=er.at[s], device_id=west, device_id_type=MESH,
            ),
        )

    def received_surface(s):
        ga = dot(LA[...], jnp.concatenate(halves(RB[s, 0]), axis=1))
        gb = dot(LB[...], jnp.concatenate(halves(RB[s, 1]), axis=1))
        ga = joined(ga)
        x = ga[0:128] + joined(gb) + pltpu.roll(ga[128:256], 96, 1)
        tiles = jnp.where(KM[...] == 0.0, x, pltpu.roll(x, 64, 1))
        spread = pltpu.roll(tiles, 0, 1, stride=16, stride_axis=0)
        out_t = []
        for t in range(2):
            keep = (big_lane // 16) == ((big_row + t) & 7)
            out_t.append(jnp.sum(jnp.where(keep, spread, 0.0).reshape(16, 8, 128), axis=1))
        return out_t[0], pltpu.roll(out_t[1], 112, 1)

    def step(s, carry):
        send_surface(s)
        copies = edge_copies(s)
        for copy in copies:
            copy.start()
        for copy in copies:
            copy.wait()
        cz, weight, cms = CO[0], CF[0], CF[5]
        columns = [EE[s, t] * CF[4] for t in range(2)]

        def advected(t, k):
            f, f_north = F[s, t, k, 0:16, :], F[s, t, k, 1:17, :]
            column = pltpu.roll(columns[t], 127 - k, 1)
            east_next = jnp.where(lane == 127, column, pltpu.roll(cz * f, 127, 1))
            return weight * f + east_next + cms * f_north

        def level(k, state):
            kappa = KAP[k]
            after = jnp.minimum(k + 1, 71)
            new = []
            for t in range(2):
                here, flux_below, edge = state[t]
                above = advected(t, after)
                flux = kappa * (above - here)
                mixed = here + flux - flux_below
                F[s + 1, t, k, 0:16, :] = mixed
                edge = jnp.where(lane == k, pltpu.roll(mixed, k, 1), edge)
                new.append((above, flux, edge))
            return tuple(new)

        def block(b, state):
            for j in range(8):
                state = level(b * 8 + j, state)
            return state

        state = tuple((advected(t, 0), zero, zero) for t in range(2))
        state = lax.fori_loop(0, 9, block, state)

        @pl.when(s == STEPS - 1)
        def _():
            pltpu.make_async_copy(
                F.at[STEPS, :, pl.ds(1, 71), pl.ds(0, 16), :], out.at[0, :, pl.ds(1, 71)], osem.at[0]
            ).start()

        pltpu.make_async_copy(RB.at[s], RB.at[s], xr.at[s]).wait()
        received = received_surface(s)
        for t in range(2):
            mixed = F[s + 1, t, 0, 0:16, :]
            surface = mixed + CF[1] * (received[t] - CP[...] * mixed)
            F[s + 1, t, 0, 0:16, :] = surface

            @pl.when(s < STEPS - 1)
            def _():
                ES[s + 1, t] = jnp.where(lane == 0, surface, state[t][2])
        return carry

    lax.fori_loop(0, STEPS, step, 0)

    last = pltpu.make_async_copy(
        F.at[STEPS, :, pl.ds(0, 1), pl.ds(0, 16), :], out.at[0, :, pl.ds(0, 1)], osem.at[1]
    )
    last.start()
    for s in range(STEPS):
        pltpu.make_async_copy(SB.at[s], SB.at[s], xs.at[s]).wait()
    pltpu.make_async_copy(
        F.at[STEPS, :, pl.ds(1, 71), pl.ds(0, 16), :], out.at[0, :, pl.ds(1, 71)], osem.at[0]
    ).wait()
    last.wait()


def local(adjoint, courant, diffusivity, coupling, partner, mask):
    any_space = pl.BlockSpec(memory_space=pl.ANY)
    vmem = pltpu.VMEM
    dma = pltpu.SemaphoreType.DMA
    return pl.pallas_call(
        kernel,
        out_shape=jax.ShapeDtypeStruct(adjoint.shape, F32),
        in_specs=[any_space] * 6,
        out_specs=any_space,
        scratch_shapes=[
            vmem((STEPS + 1, 2, 72, 24, 128), F32),
            vmem((2, 16, 128), F32),
            vmem((72, 16, 128), F32),
            vmem((16, 128), F32),
            vmem((1, 128), jnp.int32),
            vmem((16, 128), jnp.int32),
            vmem((40, 128), F32),
            vmem((40, 128), F32),
            vmem((40, 128), F32),
            vmem((16, 128), F32),
            vmem((16, 128), F32),
            vmem((24, 128), F32),
            vmem((STEPS, 2, 16, 128), F32),
            vmem((STEPS, 2, 16, 128), F32),
            vmem((STEPS, 2, 128, 128), F32),
            vmem((STEPS, 2, 128, 128), F32),
            vmem((2, 16, 128), F32),
            vmem((2, 8, 128), F32),
            vmem((128, 128), F32),
            vmem((128, 256), BF16),
            vmem((256, 128), BF16),
            vmem((256, 128), BF16),
            vmem((128, 128), BF16),
            vmem((128, 128), F32),
            vmem((6, 16, 128), F32),
            vmem((2, 8, 128), F32),
            dma((6,)),
            dma((2,)),
            dma((STEPS,)),
            dma((STEPS,)),
            dma((STEPS,)),
            dma((STEPS,)),
            dma((STEPS,)),
            dma((STEPS,)),
            dma((4,)),
            dma((4,)),
            pltpu.SemaphoreType.REGULAR,
        ],
        compiler_params=pltpu.CompilerParams(collective_id=0, has_side_effects=True),
    )(adjoint, courant, diffusivity, coupling, partner, mask)


def solution(mesh):
    placed = (
        P("mp", None, None, "lat", "lon"),
        P("mp", None, "lat", "lon"),
        P("mp", None, "lat", "lon"),
        P("mp", "lat", "lon"),
        P("mp", ("lat", "lon")),
        P("mp", "lat", "lon"),
    )
    return jax.shard_map(
        local,
        mesh=mesh,
        in_specs=placed,
        out_specs=P("mp", None, None, "lat", "lon"),
        check_vma=False,
    )
```

time: 226 us -> 88.7 us (0.39)
  blocking collectives: 86.7 us -> 0 us
  Pallas kernels: 0 us -> 84.6 us
  local copies, waits for them, and re-layouts: 72.8 us -> 2.36 us
  starting transfers between devices: 23.3 us -> 0 us
  other arithmetic: 20.7 us -> 0 us
  waiting for transfers between devices: 20.1 us -> 0 us
    all_to_all x4 -> x0, blocking collectives: 86.7 us -> none  [local(): lax.all_to_all(buffer, ('lat', 'lon'), split_axis=0, concat_axis=0, tiled...]
    pallas_call x0 -> x1, Pallas kernels: none -> 84.6 us  [local(): pl.pallas_call(kernel, out_shape=jax.ShapeDtypeStruct(adjoint.shape, F32)...]
    scatter x9 -> x0, local copies, waits for them, and re-layouts: 32.1 us -> none  [the longest x5 25.7 us: local(): fields.at[:, 0]]
    ppermute x12 -> x0, starting transfers between devices: 23.3 us -> none  [the longest x4 11 us: from_partner(): lax.ppermute(array, axis, [(i, i ^ 1 << apart) for i in range(lax.axis_si...]
    ppermute x12 -> x0, waiting for transfers between devices: 20.1 us -> none  [the longest x4 11.9 us: from_partner(): lax.ppermute(array, axis, [(i, i ^ 1 << apart) for i in range(lax.axis_si...]
    another operation x10 -> x0, local copies, waits for them, and re-layouts: 9.71 us -> none
    slice x20 -> x0, local copies, waits for them, and re-layouts: 8.72 us -> none  [the longest x4 3.21 us: local(): surface = fields[:, 0]]
    gather x8 -> x0, local copies, waits for them, and re-layouts: 7.72 us -> none  [local(): received = arrived[arrive_slot]]
  transfers between devices with their start and end apart: 12 -> 0, of which waited for: 10 -> 0; matrix products, arithmetic and copies ran while one was open for 4% -> 0% of each run, Pallas kernels for 0% -> 0%
where the time goes in v1:
time: 88.7 us; the launch traced here: 87 us
  Pallas kernels  84.6 us (95%)
  local copies, waits for them, and re-layouts  2.36 us (3%)
    pallas_call x1, Pallas kernels, local(): pl.pallas_call(kernel, out_shape=jax.ShapeDtypeStruct(adjoint.shape, F32)...  84.6 us
    unnamed x1, local copies, waits for them, and re-layouts  2.36 us

profile of v1, /device:TPU:1, one launch (start us, length us, event | category | flops | bytes accessed | tf_op | source)
XLA Modules:
  0.0 87.0 jit_solution(3980586291650021774)
XLA Ops:
  0.0 84.6 %shard_map.64 = f32[1,2,72,16,128]{4,3,2,1,0:T(8,128)} custom-call(f32[1,2,72,16,128]{4,3,2,1,0:T(8,128)} %adj.1, f32[1,2,16,128]{3,2,1,0:T(8,128)} %cour.1, f32[1,71,16,128]{3,2,1,0:T(8,128)} %diff.1, f32[1,16,128]{2,1,0:T(8,128)} %coup.1, s32[1,128]{1,0:T(1,128)} %part.1, s32[1,16,128]{2,1,0:T(8,128)} %msk.1), custom_call_target="tpu_custom_call" | custom-call | tf_op jit(solution)/shard_map/pallas_call | solution.py:329
  84.6 2.4 %copy.8 = f32[1,2,72,16,128]{4,3,2,1,0:T(8,128)} copy(f32[1,2,72,16,128]{4,3,2,1,0:T(8,128)} %shard_map.64) | data formatting | bytes 2359296

commit v2 on v1

--- a/solution.py
+++ b/solution.py
@@ -9,6 +9,7 @@
 
 TILE = 16
 STEPS = 4
+BLOCK = 12
 MESH = pl.DeviceIdType.MESH
 F32 = jnp.float32
 BF16 = jnp.bfloat16
@@ -268,27 +269,27 @@
             east_next = jnp.where(lane == 127, column, pltpu.roll(cz * f, 127, 1))
             return weight * f + east_next + cms * f_north
 
-        def level(k, state):
-            kappa = KAP[k]
-            after = jnp.minimum(k + 1, 71)
+        def block(b, state):
+            first = b * BLOCK
+            kappas = [KAP[first + j] for j in range(BLOCK)]
+            above = [
+                [advected(t, jnp.minimum(first + j + 1, 71)) for j in range(BLOCK)]
+                for t in range(2)
+            ]
             new = []
             for t in range(2):
                 here, flux_below, edge = state[t]
-                above = advected(t, after)
-                flux = kappa * (above - here)
-                mixed = here + flux - flux_below
-                F[s + 1, t, k, 0:16, :] = mixed
-                edge = jnp.where(lane == k, pltpu.roll(mixed, k, 1), edge)
-                new.append((above, flux, edge))
+                for j in range(BLOCK):
+                    flux = kappas[j] * (above[t][j] - here)
+                    mixed = here + flux - flux_below
+                    F[s + 1, t, first + j, 0:16, :] = mixed
+                    edge = jnp.where(lane == first + j, pltpu.roll(mixed, first + j, 1), edge)
+                    here, flux_below = above[t][j], flux
+                new.append((here, flux_below, edge))
             return tuple(new)
 
-        def block(b, state):
-            for j in range(8):
-                state = level(b * 8 + j, state)
-            return state
-
         state = tuple((advected(t, 0), zero, zero) for t in range(2))
-        state = lax.fori_loop(0, 9, block, state)
+        state = lax.fori_loop(0, 72 // BLOCK, block, state)
 
         @pl.when(s == STEPS - 1)
         def _():
@@ -303,6 +304,10 @@
             surface = mixed + CF[1] * (received[t] - CP[...] * mixed)
             F[s + 1, t, 0, 0:16, :] = surface
 
+            @pl.when(s == STEPS - 1)
+            def _():
+                out[0, t, 0] = surface
+
             @pl.when(s < STEPS - 1)
             def _():
                 ES[s + 1, t] = jnp.where(lane == 0, surface, state[t][2])
@@ -310,16 +315,11 @@
 
     lax.fori_loop(0, STEPS, step, 0)
 
-    last = pltpu.make_async_copy(
-        F.at[STEPS, :, pl.ds(0, 1), pl.ds(0, 16), :], out.at[0, :, pl.ds(0, 1)], osem.at[1]
-    )
-    last.start()
     for s in range(STEPS):
         pltpu.make_async_copy(SB.at[s], SB.at[s], xs.at[s]).wait()
     pltpu.make_async_copy(
         F.at[STEPS, :, pl.ds(1, 71), pl.ds(0, 16), :], out.at[0, :, pl.ds(1, 71)], osem.at[0]
     ).wait()
-    last.wait()
 
 
 def local(adjoint, courant, diffusivity, coupling, partner, mask):
@@ -328,9 +328,9 @@
     dma = pltpu.SemaphoreType.DMA
     return pl.pallas_call(
         kernel,
-        out_shape=jax.ShapeDtypeStruct(adjoint.shape, F32),
+        out_shape=vmem(adjoint.shape, F32),
         in_specs=[any_space] * 6,
-        out_specs=any_space,
+        out_specs=pl.BlockSpec(memory_space=vmem),
         scratch_shapes=[
             vmem((STEPS + 1, 2, 72, 24, 128), F32),
             vmem((2, 16, 128), F32),
@@ -359,7 +359,7 @@
             vmem((6, 16, 128), F32),
             vmem((2, 8, 128), F32),
             dma((6,)),
-            dma((2,)),
+            dma((1,)),
             dma((STEPS,)),
             dma((STEPS,)),
             dma((STEPS,)),

time: 88.7 us -> 52.5 us (0.59); the launches traced: 87 us -> 52.4 us
  Pallas kernels: 84.6 us -> 51.4 us
  local copies, waits for them, and re-layouts: 2.36 us -> 1.02 us
    pallas_call x1, Pallas kernels: 84.6 us -> 51.4 us  [local(): pl.pallas_call(kernel, out_shape=vmem(adjoint.shape, F32), in_specs=[any_...]
    unnamed x1, local copies, waits for them, and re-layouts: 2.36 us -> 1.02 us
where the time goes in v2:
time: 52.5 us; the launch traced here: 52.4 us
  Pallas kernels  51.4 us (98%)
  local copies, waits for them, and re-layouts  1.02 us (2%)
    pallas_call x1, Pallas kernels, local(): pl.pallas_call(kernel, out_shape=vmem(adjoint.shape, F32), in_specs=[any_...  51.4 us

profile of v2, /device:TPU:1, one launch (start us, length us, event | category | flops | bytes accessed | tf_op | source)
XLA Modules:
  0.0 52.4 jit_solution(1839151431117317635)
XLA Ops:
  0.0 51.4 %shard_map.64 = f32[1,2,72,16,128]{4,3,2,1,0:T(8,128)S(1)} custom-call(f32[1,2,72,16,128]{4,3,2,1,0:T(8,128)} %adj.1, f32[1,2,16,128]{3,2,1,0:T(8,128)} %cour.1, f32[1,71,16,128]{3,2,1,0:T(8,128)} %diff.1, f32[1,16,128]{2,1,0:T(8,128)} %coup.1, s32[1,128]{1,0:T(1,128)} %part.1, s32[1,16,128]{2,1,0:T(8,128)} %msk.1), custom_call_target="tpu_custom_call" | custom-call | tf_op jit(solution)/shard_map/pallas_call | solution.py:329
  51.4 1.0 %copy.8 = f32[1,2,72,16,128]{4,3,2,1,0:T(8,128)} copy(f32[1,2,72,16,128]{4,3,2,1,0:T(8,128)S(1)} %shard_map.64) | data formatting | bytes 2359296

commit v3 on v2

v3 whole, which is shorter than its diff:
```python
import functools

import jax
import jax.numpy as jnp
from jax import lax
from jax.experimental import pallas as pl
from jax.experimental.pallas import tpu as pltpu
from jax.sharding import PartitionSpec as P

TILE = 16
STEPS = 4
BLOCK = 12
MESH = pl.DeviceIdType.MESH
F32 = jnp.float32
BF16 = jnp.bfloat16


def hops(a, b, c):
    return (1 if a else 2) + min(b, 4 - b) + min(c, 8 - c)


OFFSETS = sorted(
    [(a, b, c, d) for a in range(2) for b in range(4) for c in range(8) for d in range(2)],
    key=lambda o: -hops(*o[:3]),
)


def iota(shape, axis):
    return lax.broadcasted_iota(jnp.int32, shape, axis)


def halves(x):
    high = x.astype(BF16)
    low = (x - high.astype(F32)).astype(BF16)
    return high, low


def dot(a, b):
    return jnp.dot(a, b, preferred_element_type=F32)


def kernel(
    adj, cour, diff, coup, part, msk, out,
    F, CO, KAP, CP, PT, MK, ST, STW, STS, CZE, CMN, CMS,
    ES, EE, E01, E01N, SB, RB, OHP, OHX, LR, KM, CF, ROWS, ZP,
    isem, osem, xs, xr, ns, nr, es, er, ts, tr, stage,
):
    mp, lat, lon = lax.axis_index("mp"), lax.axis_index("lat"), lax.axis_index("lon")
    me = lat * 16 + lon
    x_lo, y = lat // 4, lax.rem(lat, 4)
    z, core = lon // 2, lax.rem(lon, 2)
    east, west = (mp, lat, (lon + 1) & 15), (mp, lat, (lon + 15) & 15)
    north, south = (mp, (lat + 1) & 7, lon), (mp, (lat + 7) & 7, lon)

    loads = [
        pltpu.make_async_copy(src, dst, isem.at[i])
        for i, (src, dst) in enumerate((
            (adj.at[0, :, pl.ds(0, 2)], F.at[0, :, pl.ds(0, 2), pl.ds(0, 16), :]),
            (cour.at[0], CO),
            (part, PT),
            (diff.at[0, pl.ds(0, 1)], KAP.at[pl.ds(0, 1)]),
            (coup.at[0], CP),
            (msk.at[0], MK),
            (diff.at[0, pl.ds(1, 70)], KAP.at[pl.ds(1, 70)]),
            (adj.at[0, :, pl.ds(2, 70)], F.at[0, :, pl.ds(2, 70), pl.ds(0, 16), :]),
        ))
    ]
    bar = pltpu.get_barrier_semaphore()
    lon_peers = [(mp, lat, (lon + i) & 15) for i in (8, 9, 7, 10, 6, 11, 5, 12, 4, 13, 3, 14, 2, 15, 1)]
    lat_peers = [
        (lax.rem(mp + h, 2), (x_lo ^ a) * 4 + ((y + b) & 3), lon)
        for h in (1, 0) for a in (0, 1) for b in (2, 1, 3, 0) if h or a or b
    ]
    for peer in lat_peers + lon_peers:
        pl.semaphore_signal(bar, inc=1, device_id=peer, device_id_type=MESH)
    for load in loads:
        load.start()

    lane = iota((16, 128), 1)
    row = iota((16, 128), 0)
    sub8 = iota((8, 128), 0)
    big_lane = iota((128, 128), 1)
    big_row = iota((128, 128), 0)

    KAP[71] = jnp.zeros((16, 128), F32)
    ZP[...] = jnp.zeros((128, 128), F32)

    perm_lane = (big_lane & 15) * 8 + big_lane // 16
    perm_row = (big_row & 15) * 8 + big_row // 16
    rows_f = big_row.astype(F32)
    lanes_f = big_lane.astype(F32)

    def total(mask, values, axis):
        kept = jnp.sum(jnp.where(mask, values, 0.0), axis=axis, keepdims=True)
        return jnp.broadcast_to(kept, (128, 128))

    def remote(src, dst, send, recv, dev):
        return pltpu.make_async_remote_copy(
            src_ref=src, dst_ref=dst, send_sem=send, recv_sem=recv,
            device_id=dev, device_id_type=MESH,
        )

    def edge_copies(s):
        return (
            remote(
                F.at[s, :, :, pl.ds(0, 1), :], F.at[s, :, :, pl.ds(16, 1), :],
                ns.at[s], nr.at[s], south,
            ),
            remote(ES.at[s], EE.at[s], es.at[s], er.at[s], west),
        )

    zero = jnp.zeros((16, 128), F32)
    loads[0].wait()
    for t in range(2):
        E01[t] = jnp.where(lane == 0, F[0, t, 0, 0:16, :], pltpu.roll(F[0, t, 1, 0:16, :], 1, 1))
    loads[1].wait()
    pl.semaphore_wait(bar, 30)
    early = [
        remote(src, dst, ts.at[i], tr.at[i], dev)
        for i, (src, dst, dev) in enumerate((
            (E01, E01N, west),
            (F.at[0, :, pl.ds(0, 2), pl.ds(0, 1), :], F.at[0, :, pl.ds(0, 2), pl.ds(16, 1), :], south),
            (CO.at[0], CZE, west),
            (CO.at[1, pl.ds(0, 8)], CMN, south),
        ))
    ]
    for peer in lat_peers:
        pl.semaphore_signal(stage, inc=1, device_id=peer, device_id_type=MESH)
    for copy in early:
        copy.start()

    loads[2].wait()
    p_row = jnp.broadcast_to(PT[...], (128, 128))
    t_row, l_row = (p_row // 128).astype(F32), (p_row & 127).astype(F32)
    t_col = total(big_row == big_lane, t_row, 1)

    def sent(order):
        target = total(big_row == order, t_col, 0)
        slot = total((t_col == target) & (big_row < order), 1.0, 0)
        return target, slot

    t_send, k_send = sent(perm_lane)
    t_rev, k_rev = sent(big_lane ^ 7)
    t_from = total(big_lane == perm_row, t_row, 1)
    l_from = total(big_lane == perm_row, l_row, 1)
    KM[...] = total((t_row == t_from) & (l_row < l_from), 1.0, 1)
    loads[3].wait()
    loads[4].wait()
    a1 = CP[...] * KAP[0]
    a0 = CP[...] - a1
    ST[0:16] = a0
    ST[16:32] = a1
    ST[32:40] = jnp.where(
        sub8 == 0, t_send[0:8],
        jnp.where(sub8 == 1, k_send[0:8], jnp.where(sub8 == 2, t_rev[0:8], k_rev[0:8])),
    )
    CF[0] = 1.0 - CO[0] - CO[1]
    for half in (0, 256):
        for k in (0, 1):
            OHP[:, half + 128 * k:half + 128 * k + 128] = jnp.where(
                (t_send == rows_f) & (k_send == float(k)), 1.0, 0.0
            ).astype(BF16)
    for load in loads[5:]:
        load.wait()
    CF[1] = MK[...].astype(F32)

    def pack_level(k, edges):
        return tuple(
            jnp.where(lane == k, pltpu.roll(F[0, t, k, 0:16, :], k, 1), edges[t]) for t in range(2)
        )

    packed = lax.fori_loop(0, 72, pack_level, (zero, zero))
    ES[0, 0] = packed[0]
    ES[0, 1] = packed[1]

    later = [
        remote(src, dst, ts.at[4 + i], tr.at[4 + i], dev)
        for i, (src, dst, dev) in enumerate((
            (ES.at[0], EE.at[0], west),
            (F.at[0, :, pl.ds(2, 70), pl.ds(0, 1), :], F.at[0, :, pl.ds(2, 70), pl.ds(16, 1), :], south),
            (ST, STW, east),
            (ST, STS, north),
        ))
    ]
    for copy in later:
        copy.start()
    for copy in early:
        copy.wait()
    has_north = jnp.where(lat < 7, 1.0, 0.0)
    CF[4] = jnp.broadcast_to(CZE[:, 0:1], (16, 128))
    CMS[0:16] = CO[1]
    CMS[16:24] = jnp.broadcast_to(CMN[0:1], (8, 128)) * has_north
    CF[5] = CMS[1:17]

    def edge_columns(ref):
        return [ref[t] * CF[4] for t in range(2)]

    def advected(s, t, k, columns):
        f, f_north = F[s, t, k, 0:16, :], F[s, t, k, 1:17, :]
        column = pltpu.roll(columns[t], 127 - k, 1)
        east_next = jnp.where(lane == 127, column, pltpu.roll(CO[0] * f, 127, 1))
        return CF[0] * f + east_next + CF[5] * f_north

    def split_rows(parts):
        pairs = [halves(part) for part in parts]
        return [pair[0] for pair in pairs] + [pair[1] for pair in pairs]

    def tile_rows(own):
        parts = []
        for c in range(8):
            first = pltpu.roll(own[0], (128 - 16 * c) & 127, 1)
            second = pltpu.roll(own[1], (144 - 16 * c) & 127, 1)
            parts.append(jnp.where(lane < 16, first, jnp.where(lane < 32, second, 0.0)))
        tiles = jnp.concatenate(parts, axis=0)
        return jnp.concatenate(split_rows([tiles, pltpu.roll(tiles, 64, 1)]), axis=0)

    def pack_first():
        columns = edge_columns(E01N)
        own = []
        for t in range(2):
            own.append(ST[0:16] * advected(0, t, 0, columns) + ST[16:32] * advected(0, t, 1, columns))
        SB[0, 0] = dot(OHP[...], tile_rows(own))

    def pack(s, surfaces):
        cz, cm = CO[0], CO[1]
        edge = jnp.zeros((16, 128), F32)
        own, north_parts = [], []
        for t in range(2):
            f0, f1 = surfaces[t], F[s, t, 1, 0:16, :]
            z0, z1, m0, m1 = cz * f0, cz * f1, cm * f0, cm * f1
            value = jnp.zeros((16, 128), F32)
            for c, f, zf, mf in ((ST[0:16], f0, z0, m0), (ST[16:32], f1, z1, m1)):
                east_next = jnp.where(lane == 127, 0.0, pltpu.roll(zf, 127, 1))
                north_next = jnp.where(row == 15, 0.0, pltpu.roll(mf, 15, 0))
                value += c * (CF[0] * f + east_next + north_next)
            own.append(value)
            to_south = jnp.broadcast_to((ROWS[0] * m0[0:8] + ROWS[1] * m1[0:8])[0:1], (8, 128))
            if t:
                to_south = pltpu.roll(to_south, 16, 1)
            north_parts.append(pltpu.roll(to_south, 16, 1, stride=16, stride_axis=0))
            to_west = CF[2] * z0 + CF[3] * z1
            edge = jnp.where(lane == 15 + 16 * t, pltpu.roll(to_west, 15 + 16 * t, 1), edge)
        lanes = iota((8, 128), 1)
        both = jnp.where(lanes < 16, north_parts[0], jnp.where(lanes < 32, north_parts[1], 0.0))
        north_tiles = pltpu.roll(both, 32, 1)
        added = jnp.concatenate(
            [north_tiles, pltpu.roll(north_tiles, 64, 1), edge, pltpu.roll(edge, 64, 1), zero], axis=0
        )
        extra = jnp.concatenate(split_rows([added]), axis=0)
        SB[s, 0] = dot(OHP[...], tile_rows(own)) + dot(OHX[0:128], extra)
        SB[s, 1] = dot(OHX[128:256], extra)

    def send(s, count):
        planes = pl.ds(0, count)
        for a, b, c, d in OFFSETS:
            to_lat = (x_lo ^ a) * 4 + ((y + b) & 3)
            to_lon = ((z + c) & 7) * 2 + (core ^ d)
            remote(
                SB.at[s, planes, pl.ds(to_lat * 16 + to_lon, 1), :],
                RB.at[s, planes, pl.ds(me, 1), :],
                xs.at[s], xr.at[s], (1 - mp, to_lat, to_lon),
            ).start()

    def deep_copy():
        return pltpu.make_async_copy(
            F.at[STEPS, :, pl.ds(1, 71), pl.ds(0, 16), :], out.at[0, :, pl.ds(1, 71)], osem.at[0]
        )

    def received_surface(s):
        plane = RB[s, 0]
        parts = [plane, pltpu.roll(plane, 96, 1), RB[s, 1]]
        gathered = dot(LR[...], jnp.concatenate([half for part in parts for half in halves(part)], axis=0))
        tiles = jnp.where(KM[...] == 0.0, gathered, pltpu.roll(gathered, 64, 1))
        out_0, out_1 = zero, zero
        for c in range(8):
            moved = pltpu.roll(tiles[16 * c:16 * c + 16], 16 * c, 1)
            out_0 = jnp.where(lane // 16 == c, moved, out_0)
            out_1 = jnp.where(lane // 16 == (c + 1) % 8, moved, out_1)
        return out_0, pltpu.roll(out_1, 112, 1)

    pack_first()
    blank = pltpu.make_async_copy(ZP, RB.at[0, 1], xr.at[0])
    blank.start()
    pl.semaphore_wait(stage, 15)
    send(0, 1)
    own_rows = (t_from == lanes_f)
    north_rows = (l_from >= 120.0) & (lanes_f == t_from + 16.0)
    t_int = t_from.astype(jnp.int32)
    t_east = (t_int - (t_int & 15)) + ((t_int + 1) & 15)
    east_rows = ((l_from.astype(jnp.int32) & 7) == 7) & (big_lane == t_east)
    for i, rows in enumerate((own_rows, own_rows, north_rows, north_rows, east_rows, east_rows)):
        LR[:, 128 * i:128 * i + 128] = jnp.where(rows, 1.0, 0.0).astype(BF16)

    for copy in later:
        copy.wait()
    spread = lambda x: jnp.broadcast_to(x, (128, 128))

    def shifted_slots(ref, first, shifts, start, count):
        t_all, k_all = spread(ref[first:first + 1]), spread(ref[first + 1:first + 2])
        hit = jnp.zeros((128, 128), F32)
        for k in (0, 1):
            for half in (0, 64):
                shift = (shifts[k] + half) & 127
                inside = (big_lane >= start + count * k + half) & (big_lane < start + count * (k + 1) + half)
                found = (pltpu.roll(t_all, shift, 1) == rows_f) & (pltpu.roll(k_all, shift, 1) == float(k))
                hit = jnp.where(inside & found, 1.0, hit)
        return hit.astype(BF16)

    OHX[0:128] = shifted_slots(STS, 34, (8, 16), 0, 8)
    OHX[128:256] = shifted_slots(STW, 32, (32, 48), 16, 16)
    has_south = jnp.where(lat > 0, 1.0, 0.0)
    ROWS[0] = jnp.broadcast_to(STS[15:16], (8, 128)) * has_south
    ROWS[1] = jnp.broadcast_to(STS[31:32], (8, 128)) * has_south
    CF[2] = jnp.broadcast_to(STW[0:16, 127:128], (16, 128))
    CF[3] = jnp.broadcast_to(STW[16:32, 127:128], (16, 128))

    def step(s, carry):
        columns = edge_columns(EE.at[s])

        def block(b, state):
            first = b * BLOCK
            above = [
                [advected(s, t, jnp.minimum(first + j + 1, 71), columns) for j in range(BLOCK)]
                for t in range(2)
            ]
            new = []
            for t in range(2):
                here, flux_below, edge = state[t]
                for j in range(BLOCK):
                    flux = KAP[first + j] * (above[t][j] - here)
                    mixed = here + flux - flux_below
                    F[s + 1, t, first + j, 0:16, :] = mixed
                    edge = jnp.where(lane == first + j, pltpu.roll(mixed, first + j, 1), edge)
                    here, flux_below = above[t][j], flux
                new.append((here, flux_below, edge))
            return tuple(new)

        state = tuple((advected(s, t, 0, columns), zero, zero) for t in range(2))
        state = lax.fori_loop(0, 72 // BLOCK, block, state)

        @pl.when(s == STEPS - 1)
        def _():
            deep_copy().start()

        pltpu.make_async_copy(RB.at[s], RB.at[s], xr.at[s]).wait()
        received = received_surface(s)
        surfaces = []
        for t in range(2):
            mixed = F[s + 1, t, 0, 0:16, :]
            surfaces.append(mixed + CF[1] * (received[t] - CP[...] * mixed))

        @pl.when(s < STEPS - 1)
        def _():
            for t in range(2):
                F[s + 1, t, 0, 0:16, :] = surfaces[t]
                ES[s + 1, t] = jnp.where(lane == 0, surfaces[t], state[t][2])
            copies = edge_copies(s + 1)
            for copy in copies:
                copy.start()
            pack(s + 1, surfaces)
            send(s + 1, 2)
            for copy in copies:
                copy.wait()

        @pl.when(s == STEPS - 1)
        def _():
            for t in range(2):
                out[0, t, 0] = surfaces[t]

        return carry

    lax.fori_loop(0, STEPS, step, 0)
    for s in range(STEPS):
        gone = SB.at[s] if s else SB.at[s, 0]
        pltpu.make_async_copy(gone, gone, xs.at[s]).wait()
    deep_copy().wait()


def local(adjoint, courant, diffusivity, coupling, partner, mask):
    any_space = pl.BlockSpec(memory_space=pl.ANY)
    vmem = pltpu.VMEM
    dma = pltpu.SemaphoreType.DMA
    return pl.pallas_call(
        kernel,
        out_shape=vmem(adjoint.shape, F32),
        in_specs=[any_space] * 6,
        out_specs=pl.BlockSpec(memory_space=vmem),
        scratch_shapes=[
            vmem((STEPS + 1, 2, 72, 24, 128), F32),
            vmem((2, 16, 128), F32),
            vmem((72, 16, 128), F32),
            vmem((16, 128), F32),
            vmem((1, 128), jnp.int32),
            vmem((16, 128), jnp.int32),
            vmem((40, 128), F32),
            vmem((40, 128), F32),
            vmem((40, 128), F32),
            vmem((16, 128), F32),
            vmem((8, 128), F32),
            vmem((24, 128), F32),
            vmem((STEPS, 2, 16, 128), F32),
            vmem((STEPS, 2, 16, 128), F32),
            vmem((2, 16, 128), F32),
            vmem((2, 16, 128), F32),
            vmem((STEPS, 2, 128, 128), F32),
            vmem((STEPS, 2, 128, 128), F32),
            vmem((128, 512), BF16),
            vmem((256, 128), BF16),
            vmem((128, 768), BF16),
            vmem((128, 128), F32),
            vmem((6, 16, 128), F32),
            vmem((2, 8, 128), F32),
            vmem((128, 128), F32),
            dma((8,)),
            dma((1,)),
            dma((STEPS,)),
            dma((STEPS,)),
            dma((STEPS,)),
            dma((STEPS,)),
            dma((STEPS,)),
            dma((STEPS,)),
            dma((8,)),
            dma((8,)),
            pltpu.SemaphoreType.REGULAR,
        ],
        compiler_params=pltpu.CompilerParams(collective_id=0, has_side_effects=True),
    )(adjoint, courant, diffusivity, coupling, partner, mask)


def solution(mesh):
    placed = (
        P("mp", None, None, "lat", "lon"),
        P("mp", None, "lat", "lon"),
        P("mp", None, "lat", "lon"),
        P("mp", "lat", "lon"),
        P("mp", ("lat", "lon")),
        P("mp", "lat", "lon"),
    )
    return jax.shard_map(
        local,
        mesh=mesh,
        in_specs=placed,
        out_specs=P("mp", None, None, "lat", "lon"),
        check_vma=False,
    )
```

time: 52.5 us -> 51.7 us (0.985)
  Pallas kernels: 51.4 us -> 50.6 us
    pallas_call x1, Pallas kernels: 51.4 us -> 50.6 us  [local(): pl.pallas_call(kernel, out_shape=vmem(adjoint.shape, F32), in_specs=[any_...]
where the time goes in v3:
time: 51.7 us; the launch traced here: 51.6 us
  Pallas kernels  50.6 us (98%)
  local copies, waits for them, and re-layouts  1.02 us (2%)
    pallas_call x1, Pallas kernels, local(): pl.pallas_call(kernel, out_shape=vmem(adjoint.shape, F32), in_specs=[any_...  50.6 us

profile of v3, /device:TPU:1, one launch (start us, length us, event | category | flops | bytes accessed | tf_op | source)
XLA Modules:
  0.0 51.6 jit_solution(14356156199213869839)
XLA Ops:
  0.0 50.6 %shard_map.64 = f32[1,2,72,16,128]{4,3,2,1,0:T(8,128)S(1)} custom-call(f32[1,2,72,16,128]{4,3,2,1,0:T(8,128)} %adj.1, f32[1,2,16,128]{3,2,1,0:T(8,128)} %cour.1, f32[1,71,16,128]{3,2,1,0:T(8,128)} %diff.1, f32[1,16,128]{2,1,0:T(8,128)} %coup.1, s32[1,128]{1,0:T(1,128)} %part.1, s32[1,16,128]{2,1,0:T(8,128)} %msk.1), custom_call_target="tpu_custom_call" | custom-call | tf_op jit(solution)/shard_map/pallas_call | solution.py:383
  50.6 1.0 %copy.8 = f32[1,2,72,16,128]{4,3,2,1,0:T(8,128)} copy(f32[1,2,72,16,128]{4,3,2,1,0:T(8,128)S(1)} %shard_map.64) | data formatting | bytes 2359296

commit v4 on v3

--- a/solution.py
+++ b/solution.py
@@ -21,7 +21,7 @@
 
 OFFSETS = sorted(
     [(a, b, c, d) for a in range(2) for b in range(4) for c in range(8) for d in range(2)],
-    key=lambda o: -hops(*o[:3]),
+    key=lambda o: -(hops(o[0], o[1], 0) + 1.6 * min(o[2], 8 - o[2])),
 )
 
 
@@ -71,7 +71,7 @@
         (lax.rem(mp + h, 2), (x_lo ^ a) * 4 + ((y + b) & 3), lon)
         for h in (1, 0) for a in (0, 1) for b in (2, 1, 3, 0) if h or a or b
     ]
-    for peer in lat_peers + lon_peers:
+    for peer in lon_peers + lat_peers:
         pl.semaphore_signal(bar, inc=1, device_id=peer, device_id_type=MESH)
     for load in loads:
         load.start()
@@ -155,9 +155,9 @@
         jnp.where(sub8 == 1, k_send[0:8], jnp.where(sub8 == 2, t_rev[0:8], k_rev[0:8])),
     )
     CF[0] = 1.0 - CO[0] - CO[1]
-    for half in (0, 256):
+    for half in (0, 128):
         for k in (0, 1):
-            OHP[:, half + 128 * k:half + 128 * k + 128] = jnp.where(
+            OHP[128 * k:128 * k + 128, half:half + 128] = jnp.where(
                 (t_send == rows_f) & (k_send == float(k)), 1.0, 0.0
             ).astype(BF16)
     for load in loads[5:]:
@@ -201,25 +201,22 @@
         east_next = jnp.where(lane == 127, column, pltpu.roll(CO[0] * f, 127, 1))
         return CF[0] * f + east_next + CF[5] * f_north
 
-    def split_rows(parts):
-        pairs = [halves(part) for part in parts]
-        return [pair[0] for pair in pairs] + [pair[1] for pair in pairs]
-
-    def tile_rows(own):
+    def own_slots(own):
         parts = []
         for c in range(8):
             first = pltpu.roll(own[0], (128 - 16 * c) & 127, 1)
             second = pltpu.roll(own[1], (144 - 16 * c) & 127, 1)
             parts.append(jnp.where(lane < 16, first, jnp.where(lane < 32, second, 0.0)))
         tiles = jnp.concatenate(parts, axis=0)
-        return jnp.concatenate(split_rows([tiles, pltpu.roll(tiles, 64, 1)]), axis=0)
+        both = dot(OHP[...], jnp.concatenate(halves(tiles), axis=0))
+        return both[0:128] + pltpu.roll(both[128:256], 64, 1)
 
     def pack_first():
         columns = edge_columns(E01N)
         own = []
         for t in range(2):
             own.append(ST[0:16] * advected(0, t, 0, columns) + ST[16:32] * advected(0, t, 1, columns))
-        SB[0, 0] = dot(OHP[...], tile_rows(own))
+        SB[0, 0] = own_slots(own)
 
     def pack(s, surfaces):
         cz, cm = CO[0], CO[1]
@@ -246,8 +243,8 @@
         added = jnp.concatenate(
             [north_tiles, pltpu.roll(north_tiles, 64, 1), edge, pltpu.roll(edge, 64, 1), zero], axis=0
         )
-        extra = jnp.concatenate(split_rows([added]), axis=0)
-        SB[s, 0] = dot(OHP[...], tile_rows(own)) + dot(OHX[0:128], extra)
+        extra = jnp.concatenate(halves(added), axis=0)
+        SB[s, 0] = own_slots(own) + dot(OHX[0:128], extra)
         SB[s, 1] = dot(OHX[128:256], extra)
 
     def send(s, count):
@@ -404,7 +401,7 @@
             vmem((2, 16, 128), F32),
             vmem((STEPS, 2, 128, 128), F32),
             vmem((STEPS, 2, 128, 128), F32),
-            vmem((128, 512), BF16),
+            vmem((256, 256), BF16),
             vmem((256, 128), BF16),
             vmem((128, 768), BF16),
             vmem((128, 128), F32),

time: 51.7 us -> 51.2 us (level)
  no operation moved by 1% of the time
where the time goes in v4:
time: 51.2 us; the launch traced here: 51.1 us
  Pallas kernels  50.1 us (98%)
  local copies, waits for them, and re-layouts  1.02 us (2%)
    pallas_call x1, Pallas kernels, local(): pl.pallas_call(kernel, out_shape=vmem(adjoint.shape, F32), in_specs=[any_...  50.1 us

profile of v4, /device:TPU:1, one launch (start us, length us, event | category | flops | bytes accessed | tf_op | source)
XLA Modules:
  0.0 51.1 jit_solution(7034437877457109143)
XLA Ops:
  0.0 50.1 %shard_map.64 = f32[1,2,72,16,128]{4,3,2,1,0:T(8,128)S(1)} custom-call(f32[1,2,72,16,128]{4,3,2,1,0:T(8,128)} %adj.1, f32[1,2,16,128]{3,2,1,0:T(8,128)} %cour.1, f32[1,71,16,128]{3,2,1,0:T(8,128)} %diff.1, f32[1,16,128]{2,1,0:T(8,128)} %coup.1, s32[1,128]{1,0:T(1,128)} %part.1, s32[1,16,128]{2,1,0:T(8,128)} %msk.1), custom_call_target="tpu_custom_call" | custom-call | tf_op jit(solution)/shard_map/pallas_call | solution.py:380
  50.1 1.0 %copy.8 = f32[1,2,72,16,128]{4,3,2,1,0:T(8,128)} copy(f32[1,2,72,16,128]{4,3,2,1,0:T(8,128)S(1)} %shard_map.64) | data formatting | bytes 2359296
